TPU v7x, 768 devices: a whole 4x8x12 slice. The times are simulated.
768 devices in a mesh: tm: 24 (over x_hi, z), height: 32 (over y, x_lo, core).
Axes of the slice: x: 4 (x_hi: 2, x_lo: 2; x = x_hi * 2 + x_lo), y: 8, z: 12, core: 2. Of those that a mesh axis runs over, the one named last changes fastest.
Arguments:
- query_tok: bfloat16 [24, 64, 64, 1536], P('tm', 'height'), may hold values from -6 to 6
- key_tok: bfloat16 [24, 64, 64, 1536], P('tm', 'height'), may hold values from -6 to 6
- value_tok: bfloat16 [24, 64, 64, 1536], P('tm', 'height'), may hold values from -6 to 6
- grad_out: bfloat16 [24, 64, 64, 1536], P('tm', 'height'), may hold values from -6 to 6
- far_picks: int32 [24, 32, 12, 2], P('tm', 'height'), may hold values from 0 to 3
Outputs:
- grad_query: bfloat16 [24, 64, 64, 1536], P('tm', 'height')
- grad_key: bfloat16 [24, 64, 64, 1536], P('tm', 'height')
- grad_value: bfloat16 [24, 64, 64, 1536], P('tm', 'height')
All inputs are finite; a program needn't handle non-finite values.
Results may differ from a plain program's by a relative error of at most 0.012.
The roundings to bfloat16 on the way count: a program that leaves them out, or rounds other values in their place, can miss the bound.
Values may be sent and summed in bfloat16 or wider, within the bound.
A program may use at most 64 MiB of HBM per device.

v0:
```python
import jax
import jax.numpy as jnp
from jax import lax
from jax.sharding import PartitionSpec as P

HEAD_DIM = 128
REACH = 2


def shifted(block, axis, distance):
    devices = range(lax.axis_size(axis))
    route = [((i - distance) % len(devices), i) for i in devices]
    return lax.ppermute(block, axis, route)


def padded_2(value, sides, width):
    for axis, dim in sides:
        size, length = (lax.axis_size(axis), value.shape[dim])
        up = [(i, (i + 1) % size) for i in range(size - 1)]
        down = [(j, i) for i, j in up]
        last = lax.slice_in_dim(value, length - width, length, axis=dim)
        first = lax.slice_in_dim(value, 0, width, axis=dim)
        before = lax.ppermute(last, axis, up)
        after = lax.ppermute(first, axis, down)
        value = jnp.concatenate([before, value, after], axis=dim)
    return value


def pair_grads(query_rows, key_rows, value_rows, grad_rows, usable):
    score_scale = HEAD_DIM ** (-0.5)
    query_h = query_rows.transpose(1, 0, 2)
    key_h = key_rows.transpose(1, 0, 2)
    value_h = value_rows.transpose(1, 0, 2)
    grad_h = grad_rows.transpose(1, 0, 2)
    mask_bias = jnp.where(usable, 0.0, -jnp.inf).astype(jnp.float32)[:, None, :]
    scores = (
        jnp.einsum("hqd,hkd->hqk", query_h, key_h, preferred_element_type=jnp.float32) * score_scale
        + mask_bias
    )
    row_top = jnp.max(scores, axis=2, keepdims=True)
    expo = jnp.exp(scores - row_top)
    weights = expo / jnp.sum(expo, axis=2, keepdims=True)
    weights_b = weights.astype(jnp.bfloat16)
    attended = jnp.einsum("hqk,hkd->hqd", weights_b, value_h, preferred_element_type=jnp.float32)
    row_delta = jnp.sum(grad_h.astype(jnp.float32) * attended, axis=2)
    value_grad = jnp.einsum("hqk,hqd->hkd", weights_b, grad_h, preferred_element_type=jnp.float32)
    grad_weights = jnp.einsum("hqd,hkd->hqk", grad_h, value_h, preferred_element_type=jnp.float32)
    dscore = (weights * (grad_weights - row_delta[:, :, None]) * score_scale).astype(jnp.bfloat16)
    query_grad = jnp.einsum("hqk,hkd->hqd", dscore, key_h, preferred_element_type=jnp.float32)
    key_grad = jnp.einsum("hqk,hqd->hkd", dscore, query_h, preferred_element_type=jnp.float32)
    return (
        query_grad.transpose(1, 0, 2),
        key_grad.transpose(1, 0, 2),
        value_grad.transpose(1, 0, 2),
    )


def fetch_direct(key_value, shift_by):
    return shifted(key_value, "tm", -shift_by)


def send_back(piece, shift_by):
    return shifted(piece, "tm", shift_by)


def per_device(query_tok, key_tok, value_tok, grad_out, far_picks):
    frames_dev, rows_dev, columns, width = query_tok.shape
    tile = frames_dev * rows_dev * columns
    face = frames_dev * columns
    heads = width // HEAD_DIM
    offset_list = [shift_by for shift_by in range(-REACH, REACH + 1) if shift_by != 0]
    offset_arr = jnp.array(offset_list, dtype=jnp.int32)
    cycle_pos = lax.axis_index("tm")
    cycle_size = lax.axis_size("tm")
    key_value = jnp.concatenate([key_tok, value_tok], axis=3)
    padded = padded_2(key_value, (("height", 1),), 1)
    upper_face = padded[:, 0]
    lower_face = padded[:, rows_dev + 1]
    remote = {}
    for shift_by in offset_list:
        remote[shift_by] = fetch_direct(key_value, shift_by)
    blocks = [
        key_value.reshape(tile, 2 * width),
        upper_face.reshape(face, 2 * width),
        lower_face.reshape(face, 2 * width),
    ]
    for shift_by in offset_list:
        blocks.append(remote[shift_by].reshape(tile, 2 * width))
    stacked = jnp.concatenate(blocks, axis=0)
    total_keys = stacked.shape[0]
    line_pos = lax.axis_index("height")
    line_size = lax.axis_size("height")
    target = cycle_pos + offset_arr
    far_ok = (target >= 0) & (target < cycle_size)
    choose = jnp.arange(2 * REACH, dtype=jnp.int32)
    chosen = jnp.any(far_picks[0, 0][:, :, None] == choose, axis=1) & far_ok[None, :]
    usable = jnp.concatenate(
        [
            jnp.ones((heads, tile), jnp.bool_),
            jnp.broadcast_to(line_pos > 0, (heads, face)),
            jnp.broadcast_to(line_pos < line_size - 1, (heads, face)),
            jnp.repeat(chosen, tile, axis=1),
        ],
        axis=1,
    )
    query_grad, key_grad, value_grad = pair_grads(
        query_tok.reshape(tile, heads, HEAD_DIM),
        stacked[:, :width].reshape(total_keys, heads, HEAD_DIM),
        stacked[:, width:].reshape(total_keys, heads, HEAD_DIM),
        grad_out.reshape(tile, heads, HEAD_DIM),
        usable,
    )
    key_grads = jnp.concatenate(
        [key_grad.reshape(total_keys, width), value_grad.reshape(total_keys, width)], axis=1
    )
    own_part = key_grads[:tile].reshape(frames_dev, rows_dev, columns, 2 * width)
    face_parts = jnp.stack(
        [
            key_grads[tile : tile + face].reshape(frames_dev, columns, 2 * width),
            key_grads[tile + face : tile + 2 * face].reshape(frames_dev, columns, 2 * width),
        ],
        axis=1,
    ).astype(jnp.bfloat16)
    returned = padded_2(face_parts, (("height", 1),), 1).astype(jnp.float32)
    own_part = own_part.at[:, 0].add(returned[:, 0]).at[:, rows_dev - 1].add(returned[:, 3])
    for slot_index, shift_by in enumerate(offset_list):
        start = tile + 2 * face + slot_index * tile
        piece = (
            key_grads[start : start + tile]
            .astype(jnp.bfloat16)
            .reshape(frames_dev, rows_dev, columns, 2 * width)
        )
        own_part = own_part + send_back(piece, shift_by).astype(jnp.float32)
    grad_query = query_grad.reshape(frames_dev, rows_dev, columns, width).astype(jnp.bfloat16)
    return (
        grad_query,
        own_part[..., :width].astype(jnp.bfloat16),
        own_part[..., width:].astype(jnp.bfloat16),
    )


def solution(mesh):
    return jax.shard_map(
        per_device,
        mesh=mesh,
        in_specs=(
            P("tm", "height", None, None),
            P("tm", "height", None, None),
            P("tm", "height", None, None),
            P("tm", "height", None, None),
            P("tm", "height", None, None),
        ),
        out_specs=(
            P("tm", "height", None, None),
            P("tm", "height", None, None),
            P("tm", "height", None, None),
        ),
        check_vma=False,
    )
```

profile of v0, /device:TPU:57, one launch (start us, length us, event | category | flops | bytes accessed | tf_op | source)
XLA Modules:
  0.0 205.9 jit_solution(1412111601749360203)
XLA Ops:
  0.6 1.0 constant_dynamic-update-slice_fusion.1
  1.7 1.0 constant_dynamic-update-slice_fusion
  2.7 5.8 %collective-permute-start.2 = (bf16[1,2,64,3072]{3,2,1,0:T(8,128)(2,1)S(1)}, bf16[1,2,64,3072]{3,2,1,0:T(8,128)(2,1)}, u32[]{:S(2)}, u32[]{:S(2)}) collective-permute-start(bf16[1,2,64,3072]{3,2,1,0:T(8,128)(2,1)S(1)} %constant_dynamic-update-slice_fusion), channel_id=1, source_target_pairs={{704,0},{736,32},{0,64},{32,96},{64,128},{96,160},{128,192},{160,2... | collective-permute-start | bytes 2359304 | tf_op jit(solution)/shard_map/ppermute | solution.py:13
  8.5 4.0 %collective-permute-start.3 = (bf16[1,2,64,3072]{3,2,1,0:T(8,128)(2,1)S(1)}, bf16[1,2,64,3072]{3,2,1,0:T(8,128)(2,1)}, u32[]{:S(2)}, u32[]{:S(2)}) collective-permute-start(bf16[1,2,64,3072]{3,2,1,0:T(8,128)(2,1)S(1)} %constant_dynamic-update-slice_fusion), channel_id=1, source_target_pairs={{736,0},{0,32},{32,64},{64,96},{96,128},{128,160},{160,192},{192,2... | collective-permute-start | bytes 2359304 | tf_op jit(solution)/shard_map/ppermute | solution.py:13
  12.5 10.8 %collective-permute-start.4 = (bf16[1,2,64,3072]{3,2,1,0:T(8,128)(2,1)S(1)}, bf16[1,2,64,3072]{3,2,1,0:T(8,128)(2,1)}, u32[]{:S(2)}, u32[]{:S(2)}) collective-permute-start(bf16[1,2,64,3072]{3,2,1,0:T(8,128)(2,1)S(1)} %constant_dynamic-update-slice_fusion), channel_id=1, source_target_pairs={{32,0},{64,32},{96,64},{128,96},{160,128},{192,160},{224,192},{256... | collective-permute-start | bytes 2359304 | tf_op jit(solution)/shard_map/ppermute | solution.py:13
  23.3 4.3 %collective-permute-start.5 = (bf16[1,2,64,3072]{3,2,1,0:T(8,128)(2,1)S(1)}, bf16[1,2,64,3072]{3,2,1,0:T(8,128)(2,1)S(1)}, u32[]{:S(2)}, u32[]{:S(2)}) collective-permute-start(bf16[1,2,64,3072]{3,2,1,0:T(8,128)(2,1)S(1)} %constant_dynamic-update-slice_fusion), channel_id=1, source_target_pairs={{64,0},{96,32},{128,64},{160,96},{192,128},{224,160},{256,192},{28... | collective-permute-start | bytes 2359304 | tf_op jit(solution)/shard_map/ppermute | solution.py:13
  27.6 0.9 fusion.41
  28.5 3.6 %collective-permute-start = (bf16[1,1,64,3072]{3,2,1,0:T(8,128)(2,1)}, bf16[1,1,64,3072]{3,2,1,0:T(8,128)(2,1)}, u32[]{:S(2)}, u32[]{:S(2)}) collective-permute-start(bf16[1,1,64,3072]{3,2,1,0:T(8,128)(2,1)} %get-tuple-element.38), channel_id=1, source_target_pairs={{0,1},{1,2},{2,3},{3,4},{4,5},{5,6},{6,7},{7,8},{8,9},{9,10},{10,1... | collective-permute-start | bytes 1179656 | tf_op jit(solution)/shard_map/ppermute | solution.py:23
  32.2 0.7 fusion.36
  34.0 1.3 reshape.273
  35.6 1.3 reshape.275
  36.9 1.1 copy.65
  38.1 4.6 %collective-permute-start.1 = (bf16[1,1,64,3072]{3,2,1,0:T(8,128)(2,1)}, bf16[1,1,64,3072]{3,2,1,0:T(8,128)(2,1)S(1)}, u32[]{:S(2)}, u32[]{:S(2)}) collective-permute-start(bf16[1,1,64,3072]{3,2,1,0:T(8,128)(2,1)} %get-tuple-element.37), channel_id=1, source_target_pairs={{1,0},{2,1},{3,2},{4,3},{5,4},{6,5},{7,6},{8,7},{9,8},{10,9},{11,1... | collective-permute-start | bytes 1179656 | tf_op jit(solution)/shard_map/ppermute | solution.py:24
  42.7 1.0 bitcast_dynamic-update-slice_fusion.1
  43.7 4.8 %collective-permute-done.1 = bf16[1,1,64,3072]{3,2,1,0:T(8,128)(2,1)S(1)} collective-permute-done((bf16[1,1,64,3072]{3,2,1,0:T(8,128)(2,1)}, bf16[1,1,64,3072]{3,2,1,0:T(8,128)(2,1)S(1)}, u32[]{:S(2)}, u32[]{:S(2)}) %collective-permute-start.1) | collective-permute-done | bytes 393248 | tf_op jit(solution)/shard_map/ppermute | solution.py:24
  48.5 1.2 constant_dynamic-update-slice_fusion.5
  49.7 21.6 %collective-permute-done.3 = bf16[1,2,64,3072]{3,2,1,0:T(8,128)(2,1)} collective-permute-done((bf16[1,2,64,3072]{3,2,1,0:T(8,128)(2,1)S(1)}, bf16[1,2,64,3072]{3,2,1,0:T(8,128)(2,1)}, u32[]{:S(2)}, u32[]{:S(2)}) %collective-permute-start.3) | collective-permute-done | bytes 786464 | tf_op jit(solution)/shard_map/ppermute | solution.py:13
  71.3 1.2 constant_dynamic-update-slice_fusion.4
  72.5 1.2 constant_dynamic-update-slice_fusion.3
  73.7 1.8 fusion.39
  75.5 4.3 %copy.63 = bf16[768,1536]{0,1:T(8,128)(2,1)} copy(bf16[768,1536]{1,0:T(8,128)(2,1)} %get-tuple-element.34) | data formatting | bytes 4718592 | tf_op jit(solution)/shard_map/slice | solution.py:109
  79.8 2.5 %copy.59 = bf16[768,1536]{0,1:T(8,128)(2,1)} copy(bf16[768,1536]{1,0:T(8,128)(2,1)S(1)} %get-tuple-element.33) | data formatting | bytes 4718592 | tf_op jit(solution)/shard_map/slice | solution.py:108
  82.3 3.0 %copy.60 = bf16[768,12,128]{2,0,1:T(8,128)(2,1)S(1)} copy(bf16[768,12,128]{0,2,1:T(8,128)(2,1)} %bitcast.93) | data formatting | bytes 4718592 | tf_op jit(solution)/shard_map/reshape | solution.py:108
  85.3 0.8 fusion.12
  86.1 3.6 %fusion.42 = (f32[12,128]{1,0:T(8,128)S(1)}, f32[12,128,768]{1,2,0:T(8,128)S(1)}) fusion(f32[12,768,128]{2,1,0:T(8,128)S(1)} %fusion.12, f32[12,768]{1,0:T(8,128)S(1)} %add_select_fusion), kind=kOutput, calls=%fused_computation.67 | output fusion | flops 7078655 | bytes 9480192 | tf_op jit(solution)/shard_map/sub | solution.py:41
  90.2 0.8 copy-done.2
  90.9 2.9 %fusion.34 = f32[12,768,128]{1,2,0:T(8,128)} fusion(bf16[12,128,768]{1,2,0:T(8,128)(2,1)S(1)} %fusion.18, bf16[128,12,128]{0,2,1:T(8,128)(2,1)S(1)} %copy-done.2), kind=kOutput, calls=%fused_computation.45 | convolution fusion | flops 301989888 | bytes 7471104 | tf_op jit(solution)/shard_map/hqk,hqd->hkd/dot_general | solution.py:46
  93.9 0.8 fusion.23
  94.7 4.3 %copy.64 = bf16[768,12,128]{2,0,1:T(8,128)(2,1)} copy(bf16[768,12,128]{0,2,1:T(8,128)(2,1)} %bitcast.91) | data formatting | bytes 4718592 | tf_op jit(solution)/shard_map/reshape | solution.py:109
  99.0 4.1 %fusion.3 = bf16[12,128,768]{1,2,0:T(8,128)(2,1)S(1)} fusion(f32[12,128]{1,0:T(8,128)S(1)} %fusion.23, bf16[768,12,128]{2,0,1:T(8,128)(2,1)} %copy.64, f32[12,128,768]{1,2,0:T(8,128)} %copy-done, f32[12,128]{1,0:T(8,128)S(1)} %get-tuple-element.39, bf16[12,128,128]{2,0,1:T(8,128)(2,1)S(1)} %bitcast.95), kind=kOutput, calls=%fused_computation.11 | convolution fusion | flops 307888128 | bytes 9842688 | tf_op jit(solution)/shard_map/hqd,hkd->hqk/dot_general | solution.py:47
  103.2 0.8 fusion.24
  104.0 3.0 %fusion.43 = f32[12,768,128]{1,2,0:T(8,128)} fusion(bf16[12,128,768]{1,2,0:T(8,128)(2,1)S(1)} %fusion.3, bf16[12,128,128]{1,2,0:T(8,128)(2,1)S(1)} %copy.72), kind=kOutput, calls=%fused_computation.68 | convolution fusion | flops 301989888 | bytes 7471104 | tf_op jit(solution)/shard_map/hqk,hqd->hkd/dot_general | solution.py:50
  107.1 6.1 %copy.75 = f32[768,1536]{1,0:T(8,128)} copy(f32[768,1536]{0,1:T(8,128)} %bitcast.88) | data formatting | bytes 9437184 | tf_op jit(solution)/shard_map/reshape | solution.py:114
  113.2 6.1 %copy.74 = f32[768,1536]{1,0:T(8,128)} copy(f32[768,1536]{0,1:T(8,128)} %bitcast.89) | data formatting | bytes 9437184 | tf_op jit(solution)/shard_map/reshape | solution.py:114
  119.3 6.8 %fusion.1 = bf16[768,3072]{1,0:T(8,128)(2,1)} fusion(f32[768,1536]{1,0:T(8,128)} %copy.75, f32[768,1536]{1,0:T(8,128)} %copy.74), kind=kLoop, calls=%fused_computation.8 | loop fusion | flops 9437184 | bytes 14155776 | tf_op jit(solution)/shard_map/convert.5
  126.1 1.2 fusion.32
  127.6 1.0 convert_element_type.76
  128.6 2.2 %fusion.38 = (bf16[128,3072]{1,0:T(8,128)(2,1)S(1)}, bf16[128,3072]{1,0:T(8,128)(2,1)S(1)}, bf16[128,3072]{1,0:T(8,128)(2,1)S(1)}, bf16[128,3072]{1,0:T(8,128)(2,1)S(1)}) fusion(bf16[768,3072]{1,0:T(8,128)(2,1)} %fusion.1), kind=kLoop, calls=%fused_computation.63 | loop fusion | bytes 6291456 | tf_op jit(solution)/shard_map/slice | solution.py:129
  130.8 2.3 %collective-permute-start.11 = (bf16[1,2,64,3072]{3,2,1,0:T(8,128)(2,1)S(1)}, bf16[1,2,64,3072]{3,2,1,0:T(8,128)(2,1)S(1)}, u32[]{:S(2)}, u32[]{:S(2)}) collective-permute-start(bf16[1,2,64,3072]{3,2,1,0:T(8,128)(2,1)S(1)} %bitcast.104), channel_id=1, source_target_pairs={{704,0},{736,32},{0,64},{32,96},{64,128},{96,160},{128,192},{160,2... | collective-permute-start | bytes 2359304 | tf_op jit(solution)/shard_map/ppermute | solution.py:13
  133.2 1.9 collective-permute-start.10
  135.1 7.0 %collective-permute-start.9 = (bf16[1,2,64,3072]{3,2,1,0:T(8,128)(2,1)S(1)}, bf16[1,2,64,3072]{3,2,1,0:T(8,128)(2,1)S(1)}, u32[]{:S(2)}, u32[]{:S(2)}) collective-permute-start(bf16[1,2,64,3072]{3,2,1,0:T(8,128)(2,1)S(1)} %bitcast.102), channel_id=1, source_target_pairs={{32,0},{64,32},{96,64},{128,96},{160,128},{192,160},{224,192},{256... | collective-permute-start | bytes 2359304 | tf_op jit(solution)/shard_map/ppermute | solution.py:13
  142.1 4.8 %collective-permute-start.7 = (bf16[1,1,64,3072]{3,2,1,0:T(8,128)(2,1)S(1)}, bf16[1,1,64,3072]{3,2,1,0:T(8,128)(2,1)S(1)}, u32[]{:S(2)}, u32[]{:S(2)}) collective-permute-start(bf16[1,1,64,3072]{3,2,1,0:T(8,128)(2,1)S(1)} %bitcast.99), channel_id=1, source_target_pairs={{1,0},{2,1},{3,2},{4,3},{5,4},{6,5},{7,6},{8,7},{9,8},{10,9},{11,1... | collective-permute-start | bytes 1179656 | tf_op jit(solution)/shard_map/ppermute | solution.py:24
  146.9 4.6 %collective-permute-start.6 = (bf16[1,1,64,3072]{3,2,1,0:T(8,128)(2,1)S(1)}, bf16[1,1,64,3072]{3,2,1,0:T(8,128)(2,1)S(1)}, u32[]{:S(2)}, u32[]{:S(2)}) collective-permute-start(bf16[1,1,64,3072]{3,2,1,0:T(8,128)(2,1)S(1)} %bitcast.97), channel_id=1, source_target_pairs={{0,1},{1,2},{2,3},{3,4},{4,5},{5,6},{6,7},{7,8},{8,9},{9,10},{10,1... | collective-permute-start | bytes 1179656 | tf_op jit(solution)/shard_map/ppermute | solution.py:23
  151.6 1.2 fusion.19
  152.9 37.7 %collective-permute-done.7 = bf16[1,1,64,3072]{3,2,1,0:T(8,128)(2,1)S(1)} collective-permute-done((bf16[1,1,64,3072]{3,2,1,0:T(8,128)(2,1)S(1)}, bf16[1,1,64,3072]{3,2,1,0:T(8,128)(2,1)S(1)}, u32[]{:S(2)}, u32[]{:S(2)}) %collective-permute-start.7) | collective-permute-done | bytes 393248 | tf_op jit(solution)/shard_map/ppermute | solution.py:24
  190.6 1.9 collective-permute-start.8
  192.9 11.4 %collective-permute-done.8 = bf16[1,2,64,3072]{3,2,1,0:T(8,128)(2,1)S(1)} collective-permute-done((bf16[1,2,64,3072]{3,2,1,0:T(8,128)(2,1)S(1)}, bf16[1,2,64,3072]{3,2,1,0:T(8,128)(2,1)S(1)}, u32[]{:S(2)}, u32[]{:S(2)}) %collective-permute-start.8) | collective-permute-done | bytes 786464 | tf_op jit(solution)/shard_map/ppermute | solution.py:13
  204.9 0.9 fusion.40
  (44 shorter events, 3.5 us)
Async XLA Ops:
  2.7 45.8 %collective-permute-start.2 = (bf16[1,2,64,3072]{3,2,1,0:T(8,128)(2,1)S(1)}, bf16[1,2,64,3072]{3,2,1,0:T(8,128)(2,1)}, u32[]{:S(2)}, u32[]{:S(2)}) collective-permute-start(bf16[1,2,64,3072]{3,2,1,0:T(8,128)(2,1)S(1)} %constant_dynamic-update-slice_fusion), channel_id=1, source_target_pairs={{704,0},{736,32},{0,64},{32,96},{64,128},{96,160},{128,192},{160,2... | collective-permute-start | bytes 2359304 | tf_op jit(solution)/shard_map/ppermute | solution.py:13
  8.5 62.8 %collective-permute-start.3 = (bf16[1,2,64,3072]{3,2,1,0:T(8,128)(2,1)S(1)}, bf16[1,2,64,3072]{3,2,1,0:T(8,128)(2,1)}, u32[]{:S(2)}, u32[]{:S(2)}) collective-permute-start(bf16[1,2,64,3072]{3,2,1,0:T(8,128)(2,1)S(1)} %constant_dynamic-update-slice_fusion), channel_id=1, source_target_pairs={{736,0},{0,32},{32,64},{64,96},{96,128},{128,160},{160,192},{192,2... | collective-permute-start | bytes 2359304 | tf_op jit(solution)/shard_map/ppermute | solution.py:13
  12.5 59.9 %collective-permute-start.4 = (bf16[1,2,64,3072]{3,2,1,0:T(8,128)(2,1)S(1)}, bf16[1,2,64,3072]{3,2,1,0:T(8,128)(2,1)}, u32[]{:S(2)}, u32[]{:S(2)}) collective-permute-start(bf16[1,2,64,3072]{3,2,1,0:T(8,128)(2,1)S(1)} %constant_dynamic-update-slice_fusion), channel_id=1, source_target_pairs={{32,0},{64,32},{96,64},{128,96},{160,128},{192,160},{224,192},{256... | collective-permute-start | bytes 2359304 | tf_op jit(solution)/shard_map/ppermute | solution.py:13
  23.3 50.3 %collective-permute-start.5 = (bf16[1,2,64,3072]{3,2,1,0:T(8,128)(2,1)S(1)}, bf16[1,2,64,3072]{3,2,1,0:T(8,128)(2,1)S(1)}, u32[]{:S(2)}, u32[]{:S(2)}) collective-permute-start(bf16[1,2,64,3072]{3,2,1,0:T(8,128)(2,1)S(1)} %constant_dynamic-update-slice_fusion), channel_id=1, source_target_pairs={{64,0},{96,32},{128,64},{160,96},{192,128},{224,160},{256,192},{28... | collective-permute-start | bytes 2359304 | tf_op jit(solution)/shard_map/ppermute | solution.py:13
  28.5 9.5 %collective-permute-start = (bf16[1,1,64,3072]{3,2,1,0:T(8,128)(2,1)}, bf16[1,1,64,3072]{3,2,1,0:T(8,128)(2,1)}, u32[]{:S(2)}, u32[]{:S(2)}) collective-permute-start(bf16[1,1,64,3072]{3,2,1,0:T(8,128)(2,1)} %get-tuple-element.38), channel_id=1, source_target_pairs={{0,1},{1,2},{2,3},{3,4},{4,5},{5,6},{6,7},{7,8},{8,9},{9,10},{10,1... | collective-permute-start | bytes 1179656 | tf_op jit(solution)/shard_map/ppermute | solution.py:23
  38.1 10.4 %collective-permute-start.1 = (bf16[1,1,64,3072]{3,2,1,0:T(8,128)(2,1)}, bf16[1,1,64,3072]{3,2,1,0:T(8,128)(2,1)S(1)}, u32[]{:S(2)}, u32[]{:S(2)}) collective-permute-start(bf16[1,1,64,3072]{3,2,1,0:T(8,128)(2,1)} %get-tuple-element.37), channel_id=1, source_target_pairs={{1,0},{2,1},{3,2},{4,3},{5,4},{6,5},{7,6},{8,7},{9,8},{10,9},{11,1... | collective-permute-start | bytes 1179656 | tf_op jit(solution)/shard_map/ppermute | solution.py:24
  89.6 4.2 %copy-start = (f32[12,128,768]{1,2,0:T(8,128)}, f32[12,128,768]{1,2,0:T(8,128)S(1)}, u32[]{:S(2)}) copy-start(f32[12,128,768]{1,2,0:T(8,128)S(1)} %get-tuple-element.40) | copy-start | bytes 14155780
  89.7 1.3 copy-start.2
  90.9 3.0 %copy-start.1 = (bf16[768,1536]{0,1:T(8,128)(2,1)S(1)}, bf16[768,1536]{0,1:T(8,128)(2,1)}, u32[]{:S(2)}) copy-start(bf16[768,1536]{0,1:T(8,128)(2,1)} %copy.63) | copy-start | bytes 7077892
  113.2 12.9 %slice-start = ((s8[4718592]{0:T(1024)(128)(4,1)}), s8[524288]{0:T(1024)(128)(4,1)S(1)}, s32[]{:S(2)}) async-start(s8[4718592]{0:T(1024)(128)(4,1)} %bitcast.84), calls=%async_computation | async-start | bytes 1048576
  119.3 6.8 %slice-start.1 = ((s8[4718592]{0:T(1024)(128)(4,1)}), s8[4194304]{0:T(1024)(128)(4,1)S(1)}, s32[]{:S(2)}) async-start(s8[4718592]{0:T(1024)(128)(4,1)} %bitcast.84), calls=%async_computation.1 | async-start | bytes 8388608
  127.3 24.3 %slice-start.2 = ((s8[4718592]{0:T(1024)(128)(4,1)}), s8[524288]{0:T(1024)(128)(4,1)S(1)}, s32[]{:S(2)}) async-start(s8[4718592]{0:T(1024)(128)(4,1)} %bitcast.86), calls=%async_computation.2 | async-start | bytes 1048576
  128.6 23.0 %slice-start.3 = ((s8[4718592]{0:T(1024)(128)(4,1)}), s8[4194304]{0:T(1024)(128)(4,1)S(1)}, s32[]{:S(2)}) async-start(s8[4718592]{0:T(1024)(128)(4,1)} %bitcast.86), calls=%async_computation.3 | async-start | bytes 8388608
  130.8 62.1 %collective-permute-start.11 = (bf16[1,2,64,3072]{3,2,1,0:T(8,128)(2,1)S(1)}, bf16[1,2,64,3072]{3,2,1,0:T(8,128)(2,1)S(1)}, u32[]{:S(2)}, u32[]{:S(2)}) collective-permute-start(bf16[1,2,64,3072]{3,2,1,0:T(8,128)(2,1)S(1)} %bitcast.104), channel_id=1, source_target_pairs={{704,0},{736,32},{0,64},{32,96},{64,128},{96,160},{128,192},{160,2... | collective-permute-start | bytes 2359304 | tf_op jit(solution)/shard_map/ppermute | solution.py:13
  133.2 59.7 %collective-permute-start.10 = (bf16[1,2,64,3072]{3,2,1,0:T(8,128)(2,1)S(1)}, bf16[1,2,64,3072]{3,2,1,0:T(8,128)(2,1)S(1)}, u32[]{:S(2)}, u32[]{:S(2)}) collective-permute-start(bf16[1,2,64,3072]{3,2,1,0:T(8,128)(2,1)S(1)} %bitcast.103), channel_id=1, source_target_pairs={{736,0},{0,32},{32,64},{64,96},{96,128},{128,160},{160,192},{192,2... | collective-permute-start | bytes 2359304 | tf_op jit(solution)/shard_map/ppermute | solution.py:13
  135.1 57.8 %collective-permute-start.9 = (bf16[1,2,64,3072]{3,2,1,0:T(8,128)(2,1)S(1)}, bf16[1,2,64,3072]{3,2,1,0:T(8,128)(2,1)S(1)}, u32[]{:S(2)}, u32[]{:S(2)}) collective-permute-start(bf16[1,2,64,3072]{3,2,1,0:T(8,128)(2,1)S(1)} %bitcast.102), channel_id=1, source_target_pairs={{32,0},{64,32},{96,64},{128,96},{160,128},{192,160},{224,192},{256... | collective-permute-start | bytes 2359304 | tf_op jit(solution)/shard_map/ppermute | solution.py:13
  142.1 48.5 %collective-permute-start.7 = (bf16[1,1,64,3072]{3,2,1,0:T(8,128)(2,1)S(1)}, bf16[1,1,64,3072]{3,2,1,0:T(8,128)(2,1)S(1)}, u32[]{:S(2)}, u32[]{:S(2)}) collective-permute-start(bf16[1,1,64,3072]{3,2,1,0:T(8,128)(2,1)S(1)} %bitcast.99), channel_id=1, source_target_pairs={{1,0},{2,1},{3,2},{4,3},{5,4},{6,5},{7,6},{8,7},{9,8},{10,9},{11,1... | collective-permute-start | bytes 1179656 | tf_op jit(solution)/shard_map/ppermute | solution.py:24
  146.9 45.6 %collective-permute-start.6 = (bf16[1,1,64,3072]{3,2,1,0:T(8,128)(2,1)S(1)}, bf16[1,1,64,3072]{3,2,1,0:T(8,128)(2,1)S(1)}, u32[]{:S(2)}, u32[]{:S(2)}) collective-permute-start(bf16[1,1,64,3072]{3,2,1,0:T(8,128)(2,1)S(1)} %bitcast.97), channel_id=1, source_target_pairs={{0,1},{1,2},{2,3},{3,4},{4,5},{5,6},{6,7},{7,8},{8,9},{9,10},{10,1... | collective-permute-start | bytes 1179656 | tf_op jit(solution)/shard_map/ppermute | solution.py:23
  190.6 13.7 %collective-permute-start.8 = (bf16[1,2,64,3072]{3,2,1,0:T(8,128)(2,1)S(1)}, bf16[1,2,64,3072]{3,2,1,0:T(8,128)(2,1)S(1)}, u32[]{:S(2)}, u32[]{:S(2)}) collective-permute-start(bf16[1,2,64,3072]{3,2,1,0:T(8,128)(2,1)S(1)} %bitcast.101), channel_id=1, source_target_pairs={{64,0},{96,32},{128,64},{160,96},{192,128},{224,160},{256,192},{28... | collective-permute-start | bytes 2359304 | tf_op jit(solution)/shard_map/ppermute | solution.py:13
where the time goes:
time: 207 us; the launch traced here: 206 us
  waiting for transfers between devices  75.5 us (36%)
  starting transfers between devices  55.6 us (27%)
  local copies, waits for them, and re-layouts  45.4 us (22%)
  other arithmetic  15.9 us (8%)
  matrix products  12.5 us (6%)
    ppermute x2, waiting for transfers between devices, padded_2(): after = lax.ppermute(first, axis, down)  42.5 us
    ppermute x8, starting transfers between devices, shifted(): return lax.ppermute(block, axis, route)  38 us
    ppermute x8, waiting for transfers between devices, shifted(): return lax.ppermute(block, axis, route)  33 us
    ppermute x2, starting transfers between devices, padded_2(): after = lax.ppermute(first, axis, down)  9.46 us
    another operation x3, other arithmetic  8.61 us
    ppermute x2, starting transfers between devices, padded_2(): before = lax.ppermute(last, axis, up)  8.17 us
    unnamed x23, local copies, waits for them, and re-layouts  6.61 us
    reshape x1, local copies, waits for them, and re-layouts, per_device(): value_grad.reshape(total_keys, width)  6.13 us
  transfers between devices with their start and end apart: 12, of which 4 were waited for; matrix products, arithmetic and copies ran while one was open for 6% of the time, Pallas kernels for 0%

commit v1 on v0

v1 whole, which is shorter than its diff:
```python
import functools
import math

import jax
import jax.numpy as jnp
from jax import lax
from jax.experimental import pallas as pl
from jax.experimental.pallas import tpu as pltpu
from jax.sharding import PartitionSpec as P

HEAD_DIM = 128
MESH = pl.DeviceIdType.MESH
SCALE = HEAD_DIM ** -0.5
LOG2E = math.log2(math.e)
FAR = 1e30
REACHES = (-1, 1, -2, 2)
SLOTS = (1, 2, 0, 3)
NEAR_AT, LOCAL_AT, RELAY_AT, FAR_AT, MERGE_AT, GRAD_AT, PASS_AT, END_AT = 0, 6, 10, 13, 16, 18, 20, 22


def nt(a, b):
    return lax.dot_general(a, b, (((1,), (1,)), ((), ())), preferred_element_type=jnp.float32)


def nn(a, b):
    return lax.dot_general(a, b, (((1,), (0,)), ((), ())), preferred_element_type=jnp.float32)


def tn(a, b):
    return lax.dot_general(a, b, (((0,), (0,)), ((), ())), preferred_element_type=jnp.float32)


def flat(x):
    return x.reshape(x.shape[0] * x.shape[1], x.shape[2])


def kernel(
    sizes,
    picks, q_hbm, k_hbm, v_hbm, g_hbm,
    dq_out, dk_out, dv_out,
    qg, kv, far_qg, score, gradw, score0, gradw0,
    st_out, st_in, st_own, re_out, re_in,
    d2_out, d2_in, d1_part, d1_out, d1_in, dq_own, acc, face_out, face_in,
    load_sem, push_s, push_r, relay_s, relay_r, st_s, st_r, re_s, re_r,
    d2_s, d2_r, d1_s, d1_r, ff_s, ff_r, fb_s, fb_r,
):
    tiles_t, tiles_h, heads = sizes
    t = lax.axis_index("tm")
    h = lax.axis_index("height")
    there = [t >= 1, t <= tiles_t - 2, t >= 2, t <= tiles_t - 3]
    middle = (t >= 1) & (t <= tiles_t - 2)
    has_upper, has_lower = h >= 1, h <= tiles_h - 2
    face_there = [has_upper, has_lower]

    def tm_at(r):
        return {"tm": jnp.clip(t + r, 0, tiles_t - 1)}

    def height_at(r):
        return {"height": jnp.clip(h + r, 0, tiles_h - 1)}

    def remote(src, dst, send, recv, to):
        return pltpu.make_async_remote_copy(
            src_ref=src, dst_ref=dst, send_sem=send, recv_sem=recv, device_id=to, device_id_type=MESH
        )

    def loads(c):
        cols = pl.ds(pl.multiple_of(c * HEAD_DIM, HEAD_DIM), HEAD_DIM)
        return [
            pltpu.make_async_copy(q_hbm.at[0, :, :, cols], qg.at[c, 0], load_sem.at[0, c]),
            pltpu.make_async_copy(g_hbm.at[0, :, :, cols], qg.at[c, 1], load_sem.at[1, c]),
            pltpu.make_async_copy(k_hbm.at[0, :, :, cols], kv.at[c, 0, pl.ds(0, 2)], load_sem.at[2, c]),
            pltpu.make_async_copy(v_hbm.at[0, :, :, cols], kv.at[c, 1, pl.ds(0, 2)], load_sem.at[3, c]),
        ]

    def push(d, c):
        return remote(qg.at[c], far_qg.at[c, :, pl.ds(2 * d, 2)], push_s.at[d, c], push_r.at[d, c], tm_at(1 - 2 * d))

    def relay(d, c):
        return remote(
            far_qg.at[c, :, pl.ds(2 * d, 2)], far_qg.at[c, :, pl.ds(4 + 2 * d, 2)],
            relay_s.at[d, c], relay_r.at[d, c], tm_at(1 - 2 * d),
        )

    def stats(i, c):
        return remote(st_out.at[c, i], st_in.at[c, i ^ 1], st_s.at[i, c], st_r.at[i ^ 1, c], tm_at(REACHES[i]))

    def stats_got(i, c):
        return remote(st_out.at[c, i], st_in.at[c, i], st_s.at[i, c], st_r.at[i, c], tm_at(REACHES[i]))

    def ret(i, c):
        return remote(re_out.at[c, i], re_in.at[c, i ^ 1], re_s.at[i, c], re_r.at[i ^ 1, c], tm_at(REACHES[i]))

    def ret_got(i, c):
        return remote(re_out.at[c, i], re_in.at[c, i], re_s.at[i, c], re_r.at[i, c], tm_at(REACHES[i]))

    def dq2(d, c):
        return remote(d2_out.at[c, d], d2_in.at[c, d], d2_s.at[d, c], d2_r.at[d, c], tm_at(1 - 2 * d))

    def dq1(d, c):
        return remote(d1_out.at[c, d], d1_in.at[c, d], d1_s.at[d, c], d1_r.at[d, c], tm_at(1 - 2 * d))

    def face_push(e):
        return remote(kv.at[:, :, e], kv.at[:, :, 3 - e], ff_s.at[e], ff_r.at[1 - e], height_at(2 * e - 1))

    def face_got(e):
        return remote(kv.at[:, :, e], kv.at[:, :, 2 + e], ff_s.at[e], ff_r.at[e], height_at(2 * e - 1))

    def face_back(e, c):
        return remote(face_out.at[c, e], face_in.at[c, 1 - e], fb_s.at[e, c], fb_r.at[1 - e, c], height_at(2 * e - 1))

    def face_back_got(e, c):
        return remote(face_out.at[c, e], face_in.at[c, e], fb_s.at[e, c], fb_r.at[e, c], height_at(2 * e - 1))

    def each_head(body):
        def step(c, carry):
            body(c)
            return carry

        lax.fori_loop(0, heads, step, 0)

    @each_head
    def _(c):
        for copy in loads(c):
            copy.start()

    barrier = pltpu.get_barrier_semaphore()
    for r, ok in zip(REACHES, there):
        @pl.when(ok)
        def _():
            pl.semaphore_signal(barrier, inc=1, device_id=tm_at(r), device_id_type=MESH)
    for e in range(2):
        @pl.when(face_there[e])
        def _():
            pl.semaphore_signal(barrier, inc=1, device_id=height_at(2 * e - 1), device_id_type=MESH)

    for i in range(4):
        @pl.when(jnp.logical_not(there[i]))
        def _():
            far_qg[:, :, 2 * i : 2 * i + 2] = jnp.zeros((heads, 2, 2, 64, HEAD_DIM), jnp.bfloat16)
            st_in[:, i] = jnp.zeros((heads, 8, HEAD_DIM), jnp.float32)
            re_in[:, i] = jnp.zeros((heads, 8, HEAD_DIM), jnp.float32)
    for d in range(2):
        @pl.when(jnp.logical_not(middle))
        def _():
            d2_in[:, d] = jnp.zeros((heads, HEAD_DIM, HEAD_DIM), jnp.bfloat16)

        @pl.when(jnp.logical_not(there[d]))
        def _():
            d1_in[:, d] = jnp.zeros((heads, HEAD_DIM, HEAD_DIM), jnp.bfloat16)
    for e in range(2):
        @pl.when(jnp.logical_not(face_there[e]))
        def _():
            kv[:, :, 2 + e] = jnp.zeros((heads, 2, 64, HEAD_DIM), jnp.bfloat16)
            face_in[:, e] = jnp.zeros((heads, 2, 64, HEAD_DIM), jnp.bfloat16)

    pl.semaphore_wait(barrier, sum(ok.astype(jnp.int32) for ok in there + face_there))

    @each_head
    def _(c):
        q_load, g_load, k_load, v_load = loads(c)
        q_load.wait()
        g_load.wait()
        for d in range(2):
            @pl.when(there[1 - d])
            def _():
                push(d, c).start()

    @each_head
    def _(c):
        q_load, g_load, k_load, v_load = loads(c)
        k_load.wait()
        v_load.wait()

    for e in range(2):
        @pl.when(face_there[e])
        def _():
            face_push(e).start()

    def meet(c, first):
        rows = pl.ds(2 * first, 4)
        s = nt(flat(kv[c, 0, 0:2]), flat(far_qg[c, 0, rows])) * (SCALE * LOG2E)
        g = nt(flat(kv[c, 1, 0:2]), flat(far_qg[c, 1, rows]))
        cols = slice(first * HEAD_DIM, (first + 2) * HEAD_DIM)
        score[c, :, cols] = s
        gradw[c, :, cols] = g
        top = jnp.max(s, axis=0, keepdims=True)
        e = jnp.exp2(s - top)
        total = jnp.sum(e, axis=0, keepdims=True)
        delta = jnp.sum(e * g, axis=0, keepdims=True)
        for i in range(2):
            at = slice(i * HEAD_DIM, (i + 1) * HEAD_DIM)
            st_out[c, first + i, 0:1] = top[:, at]
            st_out[c, first + i, 1:2] = total[:, at]
            st_out[c, first + i, 2:3] = delta[:, at]

    def send_stats(c, first):
        for i in (first, first + 1):
            @pl.when(there[i])
            def _():
                stats(i, c).start()

    def stage(k, at, body):
        c = k - at

        @pl.when((c >= 0) & (c < heads))
        def _():
            body(c)

    def near(c):
        for d in range(2):
            @pl.when(there[d])
            def _():
                push(d, c).wait_recv()
        meet(c, 0)
        send_stats(c, 0)

    def send_on(c):
        for d in range(2):
            @pl.when(middle)
            def _():
                relay(d, c).start()

    def local(c):
        @pl.when(c == 0)
        def _():
            for e in range(2):
                @pl.when(face_there[e])
                def _():
                    face_got(e).wait_recv()

        s = nt(flat(kv[c, 0]), flat(qg[c, 0])) * (SCALE * LOG2E)
        g = nt(flat(kv[c, 1]), flat(qg[c, 1]))
        row = lax.broadcasted_iota(jnp.int32, s.shape, 0)
        upper_from = jnp.where(has_upper, 128, 192)
        lower_to = jnp.where(has_lower, 256, 192)
        usable = (row < 128) | ((row >= upper_from) & (row < lower_to))
        s = jnp.where(usable, s, -FAR)
        score0[c] = s
        gradw0[c] = g
        top = jnp.max(s, axis=0, keepdims=True)
        e = jnp.exp2(s - top)
        st_own[c, 0:1] = top
        st_own[c, 1:2] = jnp.sum(e, axis=0, keepdims=True)
        st_own[c, 2:3] = jnp.sum(e * g, axis=0, keepdims=True)

    def far(c):
        for d in range(2):
            @pl.when(there[2 + d])
            def _():
                relay(d, c).wait_recv()
        meet(c, 2)
        send_stats(c, 2)

    def merge(c):
        for i in range(4):
            @pl.when(there[i])
            def _():
                stats_got(i, c).wait_recv()
        off = []
        for i in range(4):
            chosen = ((picks[c, 0] == SLOTS[i]) | (picks[c, 1] == SLOTS[i])) & there[i]
            off.append(jnp.where(chosen, 0.0, FAR).astype(jnp.float32))
        tops = [st_own[c, 0:1]] + [st_in[c, i, 0:1] - off[i] for i in range(4)]
        totals = [st_own[c, 1:2]] + [st_in[c, i, 1:2] for i in range(4)]
        deltas = [st_own[c, 2:3]] + [st_in[c, i, 2:3] for i in range(4)]
        top = functools.reduce(jnp.maximum, tops)
        shares = [jnp.exp2(x - top) for x in tops]
        total = functools.reduce(jnp.add, [x * y for x, y in zip(totals, shares)])
        delta = functools.reduce(jnp.add, [x * y for x, y in zip(deltas, shares)]) / total
        lse = top + jnp.log(total) * LOG2E
        for i in range(4):
            re_out[c, i, 0:1] = lse + off[i]
            re_out[c, i, 1:2] = delta
        for i in range(4):
            @pl.when(there[i])
            def _():
                ret(i, c).start()
        w = jnp.exp2(score0[c] - lse)
        ds = (w * (gradw0[c] - delta) * SCALE).astype(jnp.bfloat16)
        value_part = nn(w.astype(jnp.bfloat16), flat(qg[c, 1]))
        key_part = nn(ds, flat(qg[c, 0]))
        dq_own[c] = tn(ds, flat(kv[c, 0]))
        acc[c, 0] = key_part[:128]
        acc[c, 1] = value_part[:128]
        for e in range(2):
            at = slice(128 + 64 * e, 192 + 64 * e)
            face_out[c, e, 0] = key_part[at].astype(jnp.bfloat16)
            face_out[c, e, 1] = value_part[at].astype(jnp.bfloat16)
        for e in range(2):
            @pl.when(face_there[e])
            def _():
                face_back(e, c).start()

    def grad(c):
        for i in range(4):
            @pl.when(there[i])
            def _():
                ret_got(i, c).wait_recv()
        ws, dss = [], []
        for i in range(4):
            at = slice(i * HEAD_DIM, (i + 1) * HEAD_DIM)
            w = jnp.exp2(score[c, :, at] - re_in[c, i, 0:1])
            ws.append(w.astype(jnp.bfloat16))
            dss.append((w * (gradw[c, :, at] - re_in[c, i, 1:2]) * SCALE).astype(jnp.bfloat16))
        w, ds = jnp.concatenate(ws, axis=1), jnp.concatenate(dss, axis=1)
        dq = tn(ds, flat(kv[c, 0, 0:2]))
        d1_part[c, 1] = dq[0:128]
        d1_part[c, 0] = dq[128:256]
        d2_out[c, 1] = dq[256:384].astype(jnp.bfloat16)
        d2_out[c, 0] = dq[384:512].astype(jnp.bfloat16)
        for d in range(2):
            @pl.when(there[3 - d])
            def _():
                dq2(d, c).start()
        acc[c, 0] += nn(ds, flat(far_qg[c, 0]))
        acc[c, 1] += nn(w, flat(far_qg[c, 1]))

    def pass_on(c):
        for d in range(2):
            @pl.when(middle)
            def _():
                dq2(d, c).wait_recv()
            d1_out[c, d] = (d1_part[c, d] + d2_in[c, d].astype(jnp.float32)).astype(jnp.bfloat16)

            @pl.when(there[1 - d])
            def _():
                dq1(d, c).start()

    def end(c):
        cols = pl.ds(pl.multiple_of(c * HEAD_DIM, HEAD_DIM), HEAD_DIM)
        for e in range(2):
            @pl.when(face_there[e])
            def _():
                face_back_got(e, c).wait_recv()
        for out, which in ((dk_out, 0), (dv_out, 1)):
            for e in range(2):
                part = acc[c, which, pl.ds(64 * e, 64)] + face_in[c, e, which].astype(jnp.float32)
                out[0, e, :, cols] = part.astype(jnp.bfloat16)
        for d in range(2):
            @pl.when(there[d])
            def _():
                dq1(d, c).wait_recv()
        dq = dq_own[c] + d1_in[c, 0].astype(jnp.float32) + d1_in[c, 1].astype(jnp.float32)
        dq_out[0, :, :, cols] = dq.astype(jnp.bfloat16).reshape(2, 64, HEAD_DIM)

    def tick(k, carry):
        stage(k, NEAR_AT, near)
        stage(k, RELAY_AT, send_on)
        stage(k, LOCAL_AT, local)
        stage(k, FAR_AT, far)
        stage(k, MERGE_AT, merge)
        stage(k, GRAD_AT, grad)
        stage(k, PASS_AT, pass_on)
        stage(k, END_AT, end)
        return carry

    lax.fori_loop(0, heads + END_AT, tick, 0)

    @each_head
    def _(c):
        for d in range(2):
            @pl.when(there[1 - d])
            def _():
                push(d, c).wait_send()
                dq1(d, c).wait_send()

            @pl.when(middle)
            def _():
                relay(d, c).wait_send()

            @pl.when(there[3 - d])
            def _():
                dq2(d, c).wait_send()

            @pl.when(face_there[d])
            def _():
                face_back(d, c).wait_send()
        for i in range(4):
            @pl.when(there[i])
            def _():
                stats(i, c).wait_send()
                ret(i, c).wait_send()

    for e in range(2):
        @pl.when(face_there[e])
        def _():
            face_push(e).wait_send()


def solution(mesh):
    tiles_t, tiles_h = mesh.shape["tm"], mesh.shape["height"]

    def per_device(query_tok, key_tok, value_tok, grad_out, far_picks):
        heads = query_tok.shape[3] // HEAD_DIM
        shape = query_tok.shape
        tile = HEAD_DIM
        bf, f32 = jnp.bfloat16, jnp.float32
        dma = pltpu.SemaphoreType.DMA
        any_spec = pl.BlockSpec(memory_space=pl.ANY)
        vmem_spec = pl.BlockSpec(memory_space=pltpu.VMEM)
        return pl.pallas_call(
            functools.partial(kernel, (tiles_t, tiles_h, heads)),
            out_shape=[jax.ShapeDtypeStruct(shape, bf)] * 3,
            in_specs=[pl.BlockSpec(memory_space=pltpu.SMEM)] + [any_spec] * 4,
            out_specs=[vmem_spec] * 3,
            scratch_shapes=[
                pltpu.VMEM((heads, 2, 2, 64, HEAD_DIM), bf),
                pltpu.VMEM((heads, 2, 4, 64, HEAD_DIM), bf),
                pltpu.VMEM((heads, 2, 8, 64, HEAD_DIM), bf),
                pltpu.VMEM((heads, tile, 4 * tile), f32),
                pltpu.VMEM((heads, tile, 4 * tile), f32),
                pltpu.VMEM((heads, 2 * tile, tile), f32),
                pltpu.VMEM((heads, 2 * tile, tile), f32),
                pltpu.VMEM((heads, 4, 8, tile), f32),
                pltpu.VMEM((heads, 4, 8, tile), f32),
                pltpu.VMEM((heads, 8, tile), f32),
                pltpu.VMEM((heads, 4, 8, tile), f32),
                pltpu.VMEM((heads, 4, 8, tile), f32),
                pltpu.VMEM((heads, 2, tile, HEAD_DIM), bf),
                pltpu.VMEM((heads, 2, tile, HEAD_DIM), bf),
                pltpu.VMEM((heads, 2, tile, HEAD_DIM), f32),
                pltpu.VMEM((heads, 2, tile, HEAD_DIM), bf),
                pltpu.VMEM((heads, 2, tile, HEAD_DIM), bf),
                pltpu.VMEM((heads, tile, HEAD_DIM), f32),
                pltpu.VMEM((heads, 2, tile, HEAD_DIM), f32),
                pltpu.VMEM((heads, 2, 2, 64, HEAD_DIM), bf),
                pltpu.VMEM((heads, 2, 2, 64, HEAD_DIM), bf),
                dma((4, heads)),
                dma((2, heads)), dma((2, heads)),
                dma((2, heads)), dma((2, heads)),
                dma((4, heads)), dma((4, heads)),
                dma((4, heads)), dma((4, heads)),
                dma((2, heads)), dma((2, heads)),
                dma((2, heads)), dma((2, heads)),
                dma((2,)), dma((2,)),
                dma((2, heads)), dma((2, heads)),
            ],
            compiler_params=pltpu.CompilerParams(
                collective_id=0, has_side_effects=True, vmem_limit_bytes=56 * 2**20
            ),
            name="tile_attention_grads",
        )(far_picks[0, 0], query_tok, key_tok, value_tok, grad_out)

    spec = P("tm", "height", None, None)
    return jax.shard_map(
        per_device, mesh=mesh, in_specs=(spec,) * 5, out_specs=(spec,) * 3, check_vma=False
    )
```

time: 207 us -> 121 us (0.58)
  the two profiles are of different devices: /device:TPU:57 before, /device:TPU:30 now
where the time goes in v1:
time: 121 us
  Pallas kernels  115 us (95%)
  local copies, waits for them, and re-layouts  5.06 us (4%)
    pallas_call x1, Pallas kernels, per_device(): pl.pallas_call(functools.partial(kernel, (tiles_t, tiles_h, heads)), out_...  115 us
    unnamed x9, local copies, waits for them, and re-layouts  4.38 us

profile of v1, /device:TPU:30, one launch (start us, length us, event | category | flops | bytes accessed | tf_op | source)
XLA Modules:
  0.0 121.0 jit_solution(5573308524464205324)
XLA Ops:
  0.6 0.0 copy-start.2
  0.6 0.7 copy-done.2
  1.3 0.7 copy.8.picks
  2.0 115.2 %tile_attention_grads.1 = (bf16[1,2,64,1536]{3,2,1,0:T(8,128)(2,1)}, bf16[1,2,64,1536]{3,2,1,0:T(8,128)(2,1)}, bf16[1,2,64,1536]{3,2,1,0:T(8,128)(2,1)}) custom-call(s32[12,2]{1,0:T(8,128)} %copy.8.picks, bf16[1,2,64,1536]{3,2,1,0:T(8,128)(2,1)} %q_hbm.1, bf16[1,2,64,1536]{3,2,1,0:T(8,128)(2,1)} %k_hbm.1, bf16[1,2,64,1536]{3,2,1,0:T(8,128)(2,1)} %v_hbm.1, ...), custom_call_target="tpu_custom_call" | custom-call | tf_op jit(solution)/shard_map/tile_attention_grads/pallas_call | solution.py:401
  117.3 0.0 copy-start.1
  117.3 1.8 %copy.12 = bf16[1,2,64,1536]{3,2,1,0:T(8,128)(2,1)} copy(bf16[1,2,64,1536]{3,2,1,0:T(8,128)(2,1)} %get-tuple-element.6) | data formatting | bytes 786432
  119.1 0.0 copy-done.1
  119.1 0.0 copy-start
  119.1 0.7 copy.13
  119.8 0.4 copy-done
  120.2 0.7 copy.14
Async XLA Ops:
  0.6 0.7 copy-start.2
  117.3 1.8 %copy-start.1 = (bf16[1,2,64,1536]{3,2,1,0:T(8,128)(2,1)S(1)}, bf16[1,2,64,1536]{3,2,1,0:T(8,128)(2,1)}, u32[]{:S(2)}) copy-start(bf16[1,2,64,1536]{3,2,1,0:T(8,128)(2,1)} %get-tuple-element.7) | copy-start | bytes 1179652
  119.1 1.1 copy-start

commit v2 on v1

--- a/solution.py
+++ b/solution.py
@@ -15,7 +15,9 @@
 FAR = 1e30
 REACHES = (-1, 1, -2, 2)
 SLOTS = (1, 2, 0, 3)
-NEAR_AT, LOCAL_AT, RELAY_AT, FAR_AT, MERGE_AT, GRAD_AT, PASS_AT, END_AT = 0, 6, 10, 13, 16, 18, 20, 22
+NEAR_AT, LOCAL_AT, RELAY_AT, FAR_AT, MERGE_AT, GRAD_AT, PASS_AT, END_AT = 0, 18, 0, 12, 24, 32, 36, 40
+FACES_AT = 4
+LATER = 8
 
 
 def nt(a, b):
@@ -40,9 +42,9 @@
     dq_out, dk_out, dv_out,
     qg, kv, far_qg, score, gradw, score0, gradw0,
     st_out, st_in, st_own, re_out, re_in,
-    d2_out, d2_in, d1_part, d1_out, d1_in, dq_own, acc, face_out, face_in,
+    d2_out, d2_in, d1_part, d1_out, d1_in, dq_own, acc, face_out, face_in, way_qg, way_dq, result,
     load_sem, push_s, push_r, relay_s, relay_r, st_s, st_r, re_s, re_r,
-    d2_s, d2_r, d1_s, d1_r, ff_s, ff_r, fb_s, fb_r,
+    d2_s, d2_r, d1_s, d1_r, ff_s, ff_r, fb_s, fb_r, way_s, way_r, ready, late, out_sem,
 ):
     tiles_t, tiles_h, heads = sizes
     t = lax.axis_index("tm")
@@ -51,6 +53,10 @@
     middle = (t >= 1) & (t <= tiles_t - 2)
     has_upper, has_lower = h >= 1, h <= tiles_h - 2
     face_there = [has_upper, has_lower]
+    low = tiles_t // 2 - 1
+    crosses = [t == low, t == low + 1]
+    ways = [tiles_t - 1, 0]
+    finals = [low + 1, low]
 
     def tm_at(r):
         return {"tm": jnp.clip(t + r, 0, tiles_t - 1)}
@@ -99,6 +105,35 @@
     def dq1(d, c):
         return remote(d1_out.at[c, d], d1_in.at[c, d], d1_s.at[d, c], d1_r.at[d, c], tm_at(1 - 2 * d))
 
+    def start(copy, kind, d, c, src, sem):
+        detour = crosses[d] & (lax.rem(c, 2) == 1)
+
+        @pl.when(jnp.logical_not(detour))
+        def _():
+            copy(d, c).start()
+
+        @pl.when(detour)
+        def _():
+            half = lax.div(c, 2)
+            remote(src, way_at(kind, half), sem, way_r.at[kind, half], {"tm": ways[d]}).start()
+
+    def way_at(kind, half):
+        return way_qg.at[half, kind] if kind < 2 else way_dq.at[half, kind - 2]
+
+    def forward(kind, d, c):
+        half = lax.div(c, 2)
+        dst, sem = (
+            (far_qg.at[c, :, pl.ds(2 * d, 2)], push_r),
+            (far_qg.at[c, :, pl.ds(4 + 2 * d, 2)], relay_r),
+            (d2_in.at[c, d], d2_r),
+            (d1_in.at[c, d], d1_r),
+        )[kind]
+        return remote(way_at(kind, half), dst, way_s.at[kind, half], sem.at[d, c], {"tm": finals[d]})
+
+    def forward_got(kind, c):
+        half = lax.div(c, 2)
+        return remote(way_at(kind, half), way_at(kind, half), way_s.at[kind, half], way_r.at[kind, half], {"tm": finals[0]})
+
     def face_push(e):
         return remote(kv.at[:, :, e], kv.at[:, :, 3 - e], ff_s.at[e], ff_r.at[1 - e], height_at(2 * e - 1))
 
@@ -124,7 +159,7 @@
             copy.start()
 
     barrier = pltpu.get_barrier_semaphore()
-    for r, ok in zip(REACHES, there):
+    for r, ok in zip(REACHES[:2], (there[0], there[1] & jnp.logical_not(crosses[0]))):
         @pl.when(ok)
         def _():
             pl.semaphore_signal(barrier, inc=1, device_id=tm_at(r), device_id_type=MESH)
@@ -132,6 +167,11 @@
         @pl.when(face_there[e])
         def _():
             pl.semaphore_signal(barrier, inc=1, device_id=height_at(2 * e - 1), device_id_type=MESH)
+    way = (t == ways[0]) | (t == ways[1])
+    for at, to in ((ways[0], low), (ways[1], low), (ways[1], low + 1), (low + 1, ways[0])):
+        @pl.when(t == at)
+        def _():
+            pl.semaphore_signal(barrier, inc=1, device_id={"tm": to}, device_id_type=MESH)
 
     for i in range(4):
         @pl.when(jnp.logical_not(there[i]))
@@ -153,28 +193,56 @@
             kv[:, :, 2 + e] = jnp.zeros((heads, 2, 64, HEAD_DIM), jnp.bfloat16)
             face_in[:, e] = jnp.zeros((heads, 2, 64, HEAD_DIM), jnp.bfloat16)
 
-    pl.semaphore_wait(barrier, sum(ok.astype(jnp.int32) for ok in there + face_there))
+    peers = [there[0] & jnp.logical_not(crosses[1]), there[1], crosses[0], crosses[0], crosses[1], t == ways[0]]
+    pl.semaphore_wait(barrier, sum(ok.astype(jnp.int32) for ok in peers + face_there))
+
+    for r, ok in zip(REACHES[:2], there[:2]):
+        @pl.when(ok & jnp.logical_not(crosses[1]))
+        def _():
+            pl.semaphore_signal(ready, inc=1, device_id=tm_at(r), device_id_type=MESH)
+    for at in (ways[1], low + 1):
+        @pl.when(crosses[0])
+        def _():
+            pl.semaphore_signal(late, inc=1, device_id={"tm": at}, device_id_type=MESH)
+
+    @each_head
+    def _(c):
+        q_load, g_load, k_load, v_load = loads(c)
+        k_load.wait()
+        v_load.wait()
+
+    def start_faces(ok):
+        for e in range(2):
+            @pl.when(face_there[e] & ok)
+            def _():
+                face_push(e).start()
+
+    yields = crosses[0] | (t == ways[0])
+    start_faces(jnp.logical_not(yields))
 
     @each_head
     def _(c):
         q_load, g_load, k_load, v_load = loads(c)
         q_load.wait()
         g_load.wait()
-        for d in range(2):
-            @pl.when(there[1 - d])
-            def _():
-                push(d, c).start()
-
-    @each_head
-    def _(c):
-        q_load, g_load, k_load, v_load = loads(c)
-        k_load.wait()
-        v_load.wait()
-
-    for e in range(2):
-        @pl.when(face_there[e])
-        def _():
-            face_push(e).start()
+
+        @pl.when(there[1])
+        def _():
+            start(push, 0, 0, c, qg.at[c], push_s.at[0, c])
+
+        @pl.when(there[0] & jnp.logical_not(crosses[1]))
+        def _():
+            start(push, 0, 1, c, qg.at[c], push_s.at[1, c])
+
+    @pl.when(crosses[1])
+    def _():
+        pl.semaphore_wait(late, 1)
+        for r in REACHES[:2]:
+            pl.semaphore_signal(ready, inc=1, device_id=tm_at(r), device_id_type=MESH)
+
+        @each_head
+        def _(c):
+            start(push, 0, 1, c, qg.at[c], push_s.at[1, c])
 
     def meet(c, first):
         rows = pl.ds(2 * first, 4)
@@ -211,6 +279,8 @@
             @pl.when(there[d])
             def _():
                 push(d, c).wait_recv()
+        if RELAY_AT == NEAR_AT:
+            send_on(c)
         meet(c, 0)
         send_stats(c, 0)
 
@@ -218,7 +288,7 @@
         for d in range(2):
             @pl.when(middle)
             def _():
-                relay(d, c).start()
+                start(relay, 1, d, c, far_qg.at[c, :, pl.ds(2 * d, 2)], relay_s.at[d, c])
 
     def local(c):
         @pl.when(c == 0)
@@ -244,6 +314,10 @@
         st_own[c, 2:3] = jnp.sum(e * g, axis=0, keepdims=True)
 
     def far(c):
+        @pl.when(c == 0)
+        def _():
+            pl.semaphore_wait(ready, sum(ok.astype(jnp.int32) for ok in there[:2]))
+
         for d in range(2):
             @pl.when(there[2 + d])
             def _():
@@ -311,7 +385,7 @@
         for d in range(2):
             @pl.when(there[3 - d])
             def _():
-                dq2(d, c).start()
+                start(dq2, 2, d, c, d2_out.at[c, d], d2_s.at[d, c])
         acc[c, 0] += nn(ds, flat(far_qg[c, 0]))
         acc[c, 1] += nn(w, flat(far_qg[c, 1]))
 
@@ -324,28 +398,81 @@
 
             @pl.when(there[1 - d])
             def _():
-                dq1(d, c).start()
+                start(dq1, 3, d, c, d1_out.at[c, d], d1_s.at[d, c])
+
+    def store(o, c):
+        cols = pl.ds(pl.multiple_of(c * HEAD_DIM, HEAD_DIM), HEAD_DIM)
+        return pltpu.make_async_copy(
+            result.at[c, o], (dq_out, dk_out, dv_out)[o].at[0, :, :, cols], out_sem.at[o, c]
+        )
+
+    def sent(c):
+        for d in range(2):
+            @pl.when(there[1 - d])
+            def _():
+                push(d, c).wait_send()
+
+            @pl.when(middle)
+            def _():
+                relay(d, c).wait_send()
+
+            @pl.when(there[3 - d])
+            def _():
+                dq2(d, c).wait_send()
+
+            @pl.when(face_there[d])
+            def _():
+                face_back(d, c).wait_send()
+        for i in range(4):
+            @pl.when(there[i])
+            def _():
+                stats(i, c).wait_send()
+                ret(i, c).wait_send()
 
     def end(c):
-        cols = pl.ds(pl.multiple_of(c * HEAD_DIM, HEAD_DIM), HEAD_DIM)
+        sent(c)
         for e in range(2):
             @pl.when(face_there[e])
             def _():
                 face_back_got(e, c).wait_recv()
-        for out, which in ((dk_out, 0), (dv_out, 1)):
+        for which in range(2):
             for e in range(2):
                 part = acc[c, which, pl.ds(64 * e, 64)] + face_in[c, e, which].astype(jnp.float32)
-                out[0, e, :, cols] = part.astype(jnp.bfloat16)
+                result[c, 1 + which, e] = part.astype(jnp.bfloat16)
+            store(1 + which, c).start()
         for d in range(2):
             @pl.when(there[d])
             def _():
                 dq1(d, c).wait_recv()
         dq = dq_own[c] + d1_in[c, 0].astype(jnp.float32) + d1_in[c, 1].astype(jnp.float32)
-        dq_out[0, :, :, cols] = dq.astype(jnp.bfloat16).reshape(2, 64, HEAD_DIM)
+        result[c, 0] = dq.astype(jnp.bfloat16).reshape(2, 64, HEAD_DIM)
+        store(0, c).start()
+
+    def on(kind, d):
+        def body(c):
+            @pl.when((t == ways[d]) & (lax.rem(c, 2) == 1))
+            def _():
+                if kind == 0 and d == 1:
+                    @pl.when(c == 1)
+                    def _():
+                        pl.semaphore_wait(late, 1)
+                forward_got(kind, c).wait_recv()
+                forward(kind, d, c).start()
+
+        return body
 
     def tick(k, carry):
+        for kind, at in enumerate((NEAR_AT, FAR_AT - 1, PASS_AT - 1, END_AT - 1)):
+            stage(k, at, on(kind, 0))
+            stage(k, at + LATER, on(kind, 1))
         stage(k, NEAR_AT, near)
-        stage(k, RELAY_AT, send_on)
+
+        @pl.when(k == FACES_AT)
+        def _():
+            start_faces(yields)
+
+        if RELAY_AT != NEAR_AT:
+            stage(k, RELAY_AT, send_on)
         stage(k, LOCAL_AT, local)
         stage(k, FAR_AT, far)
         stage(k, MERGE_AT, merge)
@@ -354,32 +481,23 @@
         stage(k, END_AT, end)
         return carry
 
-    lax.fori_loop(0, heads + END_AT, tick, 0)
+    lax.fori_loop(0, heads + END_AT + LATER, tick, 0)
 
     @each_head
     def _(c):
+        for o in range(3):
+            store(o, c).wait()
         for d in range(2):
             @pl.when(there[1 - d])
             def _():
-                push(d, c).wait_send()
                 dq1(d, c).wait_send()
 
-            @pl.when(middle)
-            def _():
-                relay(d, c).wait_send()
-
-            @pl.when(there[3 - d])
-            def _():
-                dq2(d, c).wait_send()
-
-            @pl.when(face_there[d])
-            def _():
-                face_back(d, c).wait_send()
-        for i in range(4):
-            @pl.when(there[i])
-            def _():
-                stats(i, c).wait_send()
-                ret(i, c).wait_send()
+    @each_head
+    def _(c):
+        @pl.when(way & (lax.rem(c, 2) == 1))
+        def _():
+            for kind in range(4):
+                forward(kind, 0, c).wait_send()
 
     for e in range(2):
         @pl.when(face_there[e])
@@ -397,12 +515,11 @@
         bf, f32 = jnp.bfloat16, jnp.float32
         dma = pltpu.SemaphoreType.DMA
         any_spec = pl.BlockSpec(memory_space=pl.ANY)
-        vmem_spec = pl.BlockSpec(memory_space=pltpu.VMEM)
         return pl.pallas_call(
             functools.partial(kernel, (tiles_t, tiles_h, heads)),
             out_shape=[jax.ShapeDtypeStruct(shape, bf)] * 3,
             in_specs=[pl.BlockSpec(memory_space=pltpu.SMEM)] + [any_spec] * 4,
-            out_specs=[vmem_spec] * 3,
+            out_specs=[any_spec] * 3,
             scratch_shapes=[
                 pltpu.VMEM((heads, 2, 2, 64, HEAD_DIM), bf),
                 pltpu.VMEM((heads, 2, 4, 64, HEAD_DIM), bf),
@@ -425,6 +542,9 @@
                 pltpu.VMEM((heads, 2, tile, HEAD_DIM), f32),
                 pltpu.VMEM((heads, 2, 2, 64, HEAD_DIM), bf),
                 pltpu.VMEM((heads, 2, 2, 64, HEAD_DIM), bf),
+                pltpu.VMEM((heads // 2, 2, 2, 2, 64, HEAD_DIM), bf),
+                pltpu.VMEM((heads // 2, 2, tile, HEAD_DIM), bf),
+                pltpu.VMEM((heads, 3, 2, 64, HEAD_DIM), bf),
                 dma((4, heads)),
                 dma((2, heads)), dma((2, heads)),
                 dma((2, heads)), dma((2, heads)),
@@ -434,6 +554,9 @@
                 dma((2, heads)), dma((2, heads)),
                 dma((2,)), dma((2,)),
                 dma((2, heads)), dma((2, heads)),
+                dma((4, heads // 2)), dma((4, heads // 2)),
+                pltpu.SemaphoreType.REGULAR, pltpu.SemaphoreType.REGULAR,
+                dma((3, heads)),
             ],
             compiler_params=pltpu.CompilerParams(
                 collective_id=0, has_side_effects=True, vmem_limit_bytes=56 * 2**20

time: 121 us -> 101 us (0.83)
  the two profiles are of different devices: /device:TPU:30 before, /device:TPU:34 now
where the time goes in v2:
time: 101 us; the launch traced here: 100 us
  Pallas kernels  94.4 us (93%)
  local copies, waits for them, and re-layouts  5.06 us (5%)
    pallas_call x1, Pallas kernels, per_device(): pl.pallas_call(functools.partial(kernel, (tiles_t, tiles_h, heads)), out_...  94.4 us
    unnamed x9, local copies, waits for them, and re-layouts  4.38 us

profile of v2, /device:TPU:34, one launch (start us, length us, event | category | flops | bytes accessed | tf_op | source)
XLA Modules:
  0.0 100.2 jit_solution(16373960079310581105)
XLA Ops:
  0.6 0.0 copy-start.2
  0.6 0.7 copy-done.2
  1.3 0.7 copy.8.picks
  2.0 94.4 %tile_attention_grads.1 = (bf16[1,2,64,1536]{3,2,1,0:T(8,128)(2,1)}, bf16[1,2,64,1536]{3,2,1,0:T(8,128)(2,1)}, bf16[1,2,64,1536]{3,2,1,0:T(8,128)(2,1)}) custom-call(s32[12,2]{1,0:T(8,128)} %copy.8.picks, bf16[1,2,64,1536]{3,2,1,0:T(8,128)(2,1)} %q_hbm.1, bf16[1,2,64,1536]{3,2,1,0:T(8,128)(2,1)} %k_hbm.1, bf16[1,2,64,1536]{3,2,1,0:T(8,128)(2,1)} %v_hbm.1, ...), custom_call_target="tpu_custom_call" | custom-call | tf_op jit(solution)/shard_map/tile_attention_grads/pallas_call | solution.py:518
  96.4 0.0 copy-start.1
  96.4 1.8 %copy.12 = bf16[1,2,64,1536]{3,2,1,0:T(8,128)(2,1)} copy(bf16[1,2,64,1536]{3,2,1,0:T(8,128)(2,1)} %get-tuple-element.6) | data formatting | bytes 786432
  98.3 0.0 copy-done.1
  98.3 0.0 copy-start
  98.3 0.7 copy.13
  99.0 0.4 copy-done
  99.4 0.7 copy.14
Async XLA Ops:
  0.6 0.7 copy-start.2
  96.4 1.8 %copy-start.1 = (bf16[1,2,64,1536]{3,2,1,0:T(8,128)(2,1)S(1)}, bf16[1,2,64,1536]{3,2,1,0:T(8,128)(2,1)}, u32[]{:S(2)}) copy-start(bf16[1,2,64,1536]{3,2,1,0:T(8,128)(2,1)} %get-tuple-element.7) | copy-start | bytes 1179652
  98.3 1.1 %copy-start = (bf16[1,2,64,1536]{3,2,1,0:T(8,128)(2,1)S(1)}, bf16[1,2,64,1536]{3,2,1,0:T(8,128)(2,1)}, u32[]{:S(2)}) copy-start(bf16[1,2,64,1536]{3,2,1,0:T(8,128)(2,1)} %get-tuple-element.8) | copy-start | bytes 1179652

commit v3 on v2

--- a/solution.py
+++ b/solution.py
@@ -18,6 +18,7 @@
 NEAR_AT, LOCAL_AT, RELAY_AT, FAR_AT, MERGE_AT, GRAD_AT, PASS_AT, END_AT = 0, 18, 0, 12, 24, 32, 36, 40
 FACES_AT = 4
 LATER = 8
+WAY_KINDS, ON_AT = 2, 8
 
 
 def nt(a, b):
@@ -106,6 +107,9 @@
         return remote(d1_out.at[c, d], d1_in.at[c, d], d1_s.at[d, c], d1_r.at[d, c], tm_at(1 - 2 * d))
 
     def start(copy, kind, d, c, src, sem):
+        if kind >= WAY_KINDS:
+            copy(d, c).start()
+            return
         detour = crosses[d] & (lax.rem(c, 2) == 1)
 
         @pl.when(jnp.logical_not(detour))
@@ -462,9 +466,10 @@
         return body
 
     def tick(k, carry):
-        for kind, at in enumerate((NEAR_AT, FAR_AT - 1, PASS_AT - 1, END_AT - 1)):
-            stage(k, at, on(kind, 0))
-            stage(k, at + LATER, on(kind, 1))
+        firsts = (NEAR_AT, ON_AT, PASS_AT - 1, END_AT - 1), (NEAR_AT, FAR_AT - 1, PASS_AT - 1, END_AT - 1)
+        for kind in range(WAY_KINDS):
+            stage(k, firsts[0][kind], on(kind, 0))
+            stage(k, firsts[1][kind] + LATER, on(kind, 1))
         stage(k, NEAR_AT, near)
 
         @pl.when(k == FACES_AT)
@@ -496,7 +501,7 @@
     def _(c):
         @pl.when(way & (lax.rem(c, 2) == 1))
         def _():
-            for kind in range(4):
+            for kind in range(WAY_KINDS):
                 forward(kind, 0, c).wait_send()
 
     for e in range(2):

time: 101 us -> 93.6 us (0.927)
  the two profiles are of different devices: /device:TPU:34 before, /device:TPU:28 now
where the time goes in v3:
time: 93.6 us; the launch traced here: 93.2 us
  Pallas kernels  87.5 us (93%)
  local copies, waits for them, and re-layouts  5.06 us (5%)
    pallas_call x1, Pallas kernels, per_device(): pl.pallas_call(functools.partial(kernel, (tiles_t, tiles_h, heads)), out_...  87.5 us
    unnamed x9, local copies, waits for them, and re-layouts  4.38 us

profile of v3, /device:TPU:28, one launch (start us, length us, event | category | flops | bytes accessed | tf_op | source)
XLA Modules:
  0.0 93.2 jit_solution(16954949218560426935)
XLA Ops:
  0.6 0.0 copy-start.2
  0.6 0.7 copy-done.2
  1.3 0.7 copy.8.picks
  2.0 87.5 %tile_attention_grads.1 = (bf16[1,2,64,1536]{3,2,1,0:T(8,128)(2,1)}, bf16[1,2,64,1536]{3,2,1,0:T(8,128)(2,1)}, bf16[1,2,64,1536]{3,2,1,0:T(8,128)(2,1)}) custom-call(s32[12,2]{1,0:T(8,128)} %copy.8.picks, bf16[1,2,64,1536]{3,2,1,0:T(8,128)(2,1)} %q_hbm.1, bf16[1,2,64,1536]{3,2,1,0:T(8,128)(2,1)} %k_hbm.1, bf16[1,2,64,1536]{3,2,1,0:T(8,128)(2,1)} %v_hbm.1, ...), custom_call_target="tpu_custom_call" | custom-call | tf_op jit(solution)/shard_map/tile_attention_grads/pallas_call | solution.py:523
  89.5 0.0 copy-start.1
  89.5 1.8 %copy.12 = bf16[1,2,64,1536]{3,2,1,0:T(8,128)(2,1)} copy(bf16[1,2,64,1536]{3,2,1,0:T(8,128)(2,1)} %get-tuple-element.6) | data formatting | bytes 786432
  91.3 0.0 copy-done.1
  91.3 0.0 copy-start
  91.3 0.7 copy.13
  92.1 0.4 copy-done
  92.5 0.7 copy.14
Async XLA Ops:
  0.6 0.7 copy-start.2
  89.5 1.8 %copy-start.1 = (bf16[1,2,64,1536]{3,2,1,0:T(8,128)(2,1)S(1)}, bf16[1,2,64,1536]{3,2,1,0:T(8,128)(2,1)}, u32[]{:S(2)}) copy-start(bf16[1,2,64,1536]{3,2,1,0:T(8,128)(2,1)} %get-tuple-element.7) | copy-start | bytes 1179652
  91.3 1.1 %copy-start = (bf16[1,2,64,1536]{3,2,1,0:T(8,128)(2,1)S(1)}, bf16[1,2,64,1536]{3,2,1,0:T(8,128)(2,1)}, u32[]{:S(2)}) copy-start(bf16[1,2,64,1536]{3,2,1,0:T(8,128)(2,1)} %get-tuple-element.8) | copy-start | bytes 1179652
